TPU v7x, 32 devices: a whole 2x2x4 slice. The times are simulated.
32 devices in a mesh: groups: 2 (over y), seq: 4 (over z), head: 2 (over x), sub: 2 (over core).
Axes of the slice: x: 2, y: 2, z: 4, core: 2. Of those that a mesh axis runs over, the one named last changes fastest.
Arguments:
- queries: bfloat16 [4608, 8192], P(('groups', 'seq'), ('head', 'sub')), parts along dimension 0, may hold values from -6 to 6
- keys: bfloat16 [4608, 8192], P(('groups', 'seq'), ('head', 'sub')), parts along dimension 0, may hold values from -0.0546875 to 0.0546875
- values: bfloat16 [4608, 8192], P(('groups', 'seq'), ('head', 'sub')), parts along dimension 0, may hold values from -800 to 800
- decay_exp: int32 [64], P(('head', 'sub')), may hold values from 1 to 2303, as said below
- gain: float32 [8192], P(('head', 'sub')), may hold values from 0.5 to 1.5
Outputs:
- normed: bfloat16 [4608, 8192], P(('groups', 'seq'), ('head', 'sub')), parts along dimension 0
- final_state: float32 [128, 128, 128], P(('groups', 'head', 'sub'), 'seq'), parts along dimension 0
There are 2 independent parts, one for each index of `groups`. A program takes and returns all parts, laid end to end along the dimension named above; an argument that names none is the same for every part. Nothing has to cross between parts.
Inputs may be any that keep to these rules, and one draw needn't show every extreme that they name: The decay of head h over one position is 2 ** (-decay_exp[h] / 18432).
All inputs are finite; a program needn't handle non-finite values.
Results may differ from a plain program's by a relative error of at most 0.0049.
Values sent between devices are 32-bit elements; how exact they have to be, the bound alone decides.
A program may use at most 64 MiB of HBM per device.

v0:
```python
import jax
import jax.numpy as jnp
from jax import lax
from jax.sharding import PartitionSpec as P

HEADS = 64
DK = 128


def local(queries, keys, values, decay_exp, gain):
    tokens = queries.shape[0]
    heads_here = decay_exp.shape[0]
    head_size = queries.shape[1] // heads_here
    n_seq = lax.axis_size("seq")
    decay_rate = decay_exp.astype(jnp.float32) / (8.0 * tokens * n_seq)
    offsets = jnp.arange(tokens).astype(jnp.float32)
    distance = offsets[:, None] - offsets[None, :]
    causal = distance >= 0
    within = jnp.where(
        causal[None], jnp.exp2(-decay_rate[:, None, None] * jnp.maximum(distance, 0.0)[None]), 0.0
    )
    key_decay = jnp.exp2(-decay_rate[None, :] * (tokens - 1.0 - offsets)[:, None])
    query_decay = jnp.exp2(-decay_rate[None, :] * (offsets + 1.0)[:, None])
    query_heads = queries.reshape(tokens, heads_here, head_size)
    key_heads = keys.reshape(tokens, heads_here, head_size)
    value_heads = values.reshape(tokens, heads_here, head_size)
    scaled_keys = (key_heads.astype(jnp.float32) * key_decay[:, :, None]).astype(jnp.bfloat16)
    local_state = jnp.einsum(
        "ihd,ihe->hde", scaled_keys, value_heads, preferred_element_type=jnp.float32
    )
    row_pieces = lax.all_to_all(local_state[None], "seq", split_axis=2, concat_axis=0, tiled=True)
    ranks = jnp.arange(n_seq).astype(jnp.float32)
    gap = ranks[:, None] - 1.0 - ranks[None, :]
    prior = jnp.where(
        gap[:, :, None] >= 0,
        jnp.exp2(-decay_rate[None, None, :] * tokens * jnp.maximum(gap, 0.0)[:, :, None]),
        0.0,
    )
    toward_end = jnp.exp2(-decay_rate[None, :] * tokens * (n_seq - 1.0 - ranks)[:, None])
    prefix_by_block = jnp.einsum(
        "bmh,mhre->bhre", prior, row_pieces, precision=lax.Precision.HIGHEST
    )
    final_rows = jnp.einsum("mh,mhre->hre", toward_end, row_pieces, precision=lax.Precision.HIGHEST)
    prefix = lax.all_to_all(prefix_by_block, "seq", split_axis=0, concat_axis=2, tiled=True)[0]
    scores = jnp.einsum("ihd,jhd->hij", query_heads, key_heads, preferred_element_type=jnp.float32)
    weights = (scores * within).astype(jnp.bfloat16)
    intra = jnp.einsum("hij,jhd->ihd", weights, value_heads, preferred_element_type=jnp.float32)
    decayed_query = query_heads.astype(jnp.float32) * query_decay[:, :, None]
    inter = jnp.einsum("ihd,hde->ihe", decayed_query, prefix, precision=lax.Precision.HIGHEST)
    mixed = (intra + inter).reshape(tokens, heads_here * head_size)
    squares = jnp.sum(mixed * mixed, axis=1)
    summed = lax.psum(squares, ("head", "sub"))
    mean_square = summed / (HEADS * DK)
    normed = (mixed * lax.rsqrt(mean_square + 1e-06)[:, None] * gain[None, :]).astype(jnp.bfloat16)
    return (normed, final_rows)


def solution(mesh):
    return jax.shard_map(
        local,
        mesh=mesh,
        in_specs=(
            P(("groups", "seq"), ("head", "sub")),
            P(("groups", "seq"), ("head", "sub")),
            P(("groups", "seq"), ("head", "sub")),
            P(("head", "sub")),
            P(("head", "sub")),
        ),
        out_specs=(
            P(("groups", "seq"), ("head", "sub")),
            P(("groups", "head", "sub"), "seq", None),
        ),
        check_vma=False,
    )
```

profile of v0, /device:TPU:0, one launch (start us, length us, event | category | flops | bytes accessed | tf_op | source)
XLA Modules:
  0.0 92.8 jit_solution(15200276459177829985)
XLA Ops:
  0.6 0.0 copy-start
  0.7 0.8 broadcast_multiply_fusion
  1.5 0.1 multiply_exponential_fusion
  1.6 4.7 %fusion.30 = f32[1,16,128,128]{3,2,1,0:T(8,128)S(1)} fusion(f32[576,16]{0,1:T(8,128)S(1)} %get-tuple-element.3, bf16[576,2048]{1,0:T(8,128)(2,1)} %param.7, bf16[576,2048]{1,0:T(8,128)(2,1)} %param.6), kind=kOutput, calls=%fused_computation.30 | convolution fusion | flops 305528832 | bytes 5804032 | tf_op jit(solution)/shard_map/ihd,ihe->hde/dot_general | solution.py:28
  6.3 1.6 %copy.34 = f32[1,16,128,128]{3,1,0,2:T(8,128)} copy(f32[1,16,128,128]{3,2,1,0:T(8,128)S(1)} %fusion.30) | data formatting | bytes 2097152 | tf_op jit(solution)/shard_map/broadcast_in_dim | solution.py:31
  7.8 6.3 %all-to-all-start = ((f32[1,16,128,128]{3,1,0,2:T(8,128)}), f32[1,16,128,128]{3,1,0,2:T(8,128)S(1)}, u32[]{:S(2)}, u32[]{:S(2)}) async-start(f32[1,16,128,128]{3,1,0,2:T(8,128)} %copy.34), calls=%async_computation | async-start | bytes 2097152 | tf_op jit(solution)/shard_map/all_to_all | solution.py:31
  14.2 0.1 exponential_bitcast_fusion
  14.3 0.1 copy.42
  14.4 0.1 subtract_compare_fusion.1
  14.4 0.1 subtract_maximum_fusion.1
  14.5 1.1 %subtract_compare_fusion = pred[576,576]{1,0:T(8,128)(4,1)} fusion(f32[576]{0:T(1024)S(1)} %iota_convert_fusion), kind=kLoop, calls=%fused_computation.23 | loop fusion | flops 663552 | bytes 334080 | tf_op jit(solution)/shard_map/ge | solution.py:18
  15.6 1.3 %subtract_maximum_fusion = f32[576,576]{1,0:T(8,128)} fusion(f32[576]{0:T(1024)S(1)} %iota_convert_fusion), kind=kLoop, calls=%fused_computation.22 | loop fusion | flops 663552 | bytes 1329408 | tf_op jit(solution)/shard_map/max | solution.py:20
  16.9 23.1 %all-to-all-done = f32[1,16,128,128]{3,1,0,2:T(8,128)S(1)} async-done(((f32[1,16,128,128]{3,1,0,2:T(8,128)}), f32[1,16,128,128]{3,1,0,2:T(8,128)S(1)}, u32[]{:S(2)}, u32[]{:S(2)}) %all-to-all-start) | async-done | bytes 1048608 | tf_op jit(solution)/shard_map/all_to_all | solution.py:31
  39.9 2.5 %convolution_bitcast_fusion = f32[4,16,32,128]{3,0,2,1:T(4,128)S(1)} fusion(f32[1,16,4,32,128]{4,1,3,2,0:T(8,128)S(1)} %bitcast.93, f32[4,4]{1,0:T(4,128)S(1)} %subtract_maximum_fusion.1, f32[16]{0:T(128)S(1)} %get-tuple-element.4, pred[4,4]{1,0:T(4,128)(4,1)S(1)} %subtract_compare_fusion.1), kind=kOutput, calls=%fused_computation.31 | convolution fusion | flops 12583680 | bytes 2097296 | tf_op jit(solution)/shard_map/bmh,mhre->bhre/dot_general | solution.py:40
  42.4 1.1 %copy.37 = f32[4,16,32,128]{3,2,1,0:T(8,128)} copy(f32[4,16,32,128]{3,0,2,1:T(4,128)S(1)} %convolution_bitcast_fusion) | data formatting | bytes 2097152 | tf_op jit(solution)/shard_map/bmh,mhre->bhre/transpose | solution.py:40
  43.6 4.4 %all-to-all-start.1 = ((f32[4,16,32,128]{3,2,1,0:T(8,128)}), f32[4,16,32,128]{3,2,1,0:T(8,128)}, u32[]{:S(2)}, u32[]{:S(2)}) async-start(f32[4,16,32,128]{3,2,1,0:T(8,128)} %copy.37), calls=%async_computation.1 | async-start | bytes 2097152 | tf_op jit(solution)/shard_map/all_to_all | solution.py:44
  48.0 0.0 copy-done
  48.1 12.4 %fusion = f32[16,576,128]{2,1,0:T(8,128)} fusion(f32[576,576]{1,0:T(8,128)} %subtract_maximum_fusion, f32[16]{0:T(128)S(1)} %get-tuple-element.5, pred[576,576]{1,0:T(8,128)(4,1)} %subtract_compare_fusion, bf16[576,2048]{1,0:T(8,128)(2,1)} %param.7, bf16[576,2048]{1,0:T(8,128)(2,1)} %param.6, bf16[576,2048]{1,0:T(8,128)(2,1)S(1)} %copy-done), kind=kOutput, calls=%fused_computation.1 | convolution fusion | flops 2744451072 | bytes 13455424 | tf_op jit(solution)/shard_map/hij,jhd->ihd/dot_general | solution.py:47
  60.5 3.1 %fusion.33 = f32[16,1,32,128]{3,1,2,0:T(1,128)} fusion(f32[4,16,1,1]{0,2,3,1:T(1,128)S(1)} %copy.42, f32[1,16,4,32,128]{4,1,3,2,0:T(8,128)S(1)} %bitcast.94), kind=kOutput, calls=%fused_computation.32 | convolution fusion | flops 3145728 | bytes 1310976 | tf_op jit(solution)/shard_map/mh,mhre->hre/dot_general | solution.py:43
  63.6 9.6 %all-to-all-done.1 = f32[4,16,32,128]{3,2,1,0:T(8,128)} async-done(((f32[4,16,32,128]{3,2,1,0:T(8,128)}), f32[4,16,32,128]{3,2,1,0:T(8,128)}, u32[]{:S(2)}, u32[]{:S(2)}) %all-to-all-start.1) | async-done | bytes 1048608 | tf_op jit(solution)/shard_map/all_to_all | solution.py:44
  73.2 1.3 %copy.38 = f32[4,16,32,128]{3,2,0,1:T(8,128)S(1)} copy(f32[4,16,32,128]{3,2,1,0:T(8,128)} %all-to-all-done.1) | data formatting | bytes 2097152 | tf_op jit(solution)/shard_map/all_to_all | solution.py:44
  74.5 0.0 copy-start.1
  74.5 8.2 %multiply_reduce_fusion = (f32[576]{0:T(1024)S(1)}, f32[576,16,128]{2,0,1:T(8,128)}) fusion(f32[16,128,128]{2,1,0:T(8,128)S(1)} %bitcast.95, f32[576,16]{0,1:T(8,128)S(1)} %get-tuple-element.2, f32[16,576,128]{2,1,0:T(8,128)} %fusion, bf16[576,2048]{1,0:T(8,128)(2,1)S(1)} %copy-done), kind=kOutput, calls=%fused_computation.8 | convolution fusion | flops 1817837056 | bytes 12884224 | tf_op jit(solution)/shard_map/ihd,hde->ihe/dot_general | solution.py:49
  82.7 5.8 %psum.7 = f32[576]{0:T(1024)S(1)} all-reduce(f32[576]{0:T(1024)S(1)} %get-tuple-element.6), channel_id=1, replica_groups=mesh['groups'=2,'seq'=4,'head'=2,'sub'=2] {'head','sub'}, use_global_device_ids=true, to_apply=%region_1.2 | all-reduce | flops 576 | bytes 4608 | tf_op jit(solution)/shard_map/psum | solution.py:52
  88.6 0.0 copy-done.1
  88.6 4.2 %fusion.5 = bf16[576,2048]{1,0:T(8,128)(2,1)} fusion(f32[2048]{0:T(1024)S(1)} %copy-done.1, f32[576]{0:T(1024)S(1)} %add_rsqrt_fusion, f32[576,16,128]{2,0,1:T(8,128)} %get-tuple-element.7), kind=kLoop, calls=%fused_computation.6 | loop fusion | flops 3538944 | bytes 7088384 | tf_op jit(solution)/shard_map/convert_element_type | solution.py:54
  (6 shorter events, 0.0 us)
Async XLA Ops:
  0.6 47.4 %copy-start = (bf16[576,2048]{1,0:T(8,128)(2,1)S(1)}, bf16[576,2048]{1,0:T(8,128)(2,1)}, u32[]{:S(2)}) copy-start(bf16[576,2048]{1,0:T(8,128)(2,1)} %param.5) | copy-start | bytes 7077892
  7.8 32.1 %all-to-all-start = ((f32[1,16,128,128]{3,1,0,2:T(8,128)}), f32[1,16,128,128]{3,1,0,2:T(8,128)S(1)}, u32[]{:S(2)}, u32[]{:S(2)}) async-start(f32[1,16,128,128]{3,1,0,2:T(8,128)} %copy.34), calls=%async_computation | async-start | bytes 2097152 | tf_op jit(solution)/shard_map/all_to_all | solution.py:31
  43.6 29.6 %all-to-all-start.1 = ((f32[4,16,32,128]{3,2,1,0:T(8,128)}), f32[4,16,32,128]{3,2,1,0:T(8,128)}, u32[]{:S(2)}, u32[]{:S(2)}) async-start(f32[4,16,32,128]{3,2,1,0:T(8,128)} %copy.37), calls=%async_computation.1 | async-start | bytes 2097152 | tf_op jit(solution)/shard_map/all_to_all | solution.py:44
  74.5 14.1 %copy-start.1 = (f32[2048]{0:T(1024)S(1)}, f32[2048]{0:T(1024)}, u32[]{:S(2)}) copy-start(f32[2048]{0:T(1024)} %param.9) | copy-start | bytes 24580
where the time goes:
time: 93.2 us; the launch traced here: 92.8 us
  waiting for transfers between devices  32.7 us (35%)
  matrix products  31 us (33%)
  starting transfers between devices  10.8 us (12%)
  other arithmetic  7.7 us (8%)
  blocking collectives  5.83 us (6%)
  local copies, waits for them, and re-layouts  4.14 us (4%)
    all_to_all x1, waiting for transfers between devices, local(): lax.all_to_all(local_state[None], 'seq', split_axis=2, concat_axis=0, til...  23.1 us
    dot_general x1, matrix products, local(): jnp.einsum('hij,jhd->ihd', weights, value_heads, preferred_element_type=j...  12.4 us
    all_to_all x1, waiting for transfers between devices, local(): lax.all_to_all(prefix_by_block, 'seq', split_axis=0, concat_axis=2, tiled...  9.61 us
    dot_general x1, matrix products, local(): jnp.einsum('ihd,hde->ihe', decayed_query, prefix, precision=lax.Precision...  8.2 us
    all_to_all x1, starting transfers between devices, local(): lax.all_to_all(local_state[None], 'seq', split_axis=2, concat_axis=0, til...  6.35 us
    psum x1, blocking collectives, local(): summed = lax.psum(squares, ('head', 'sub'))  5.83 us
    dot_general x1, matrix products, local(): jnp.einsum('ihd,ihe->hde', scaled_keys, value_heads, preferred_element_ty...  4.7 us
    all_to_all x1, starting transfers between devices, local(): lax.all_to_all(prefix_by_block, 'seq', split_axis=0, concat_axis=2, tiled...  4.44 us
  transfers between devices with their start and end apart: 2, of which 2 were waited for; matrix products, arithmetic and copies ran while one was open for 20% of the time, Pallas kernels for 0%

commit v1 on v0

--- a/solution.py
+++ b/solution.py
@@ -49,7 +49,8 @@
     inter = jnp.einsum("ihd,hde->ihe", decayed_query, prefix, precision=lax.Precision.HIGHEST)
     mixed = (intra + inter).reshape(tokens, heads_here * head_size)
     squares = jnp.sum(mixed * mixed, axis=1)
-    summed = lax.psum(squares, ("head", "sub"))
+    parts = lax.all_gather(squares, ("head", "sub"))
+    summed = jnp.sum(parts, axis=0)
     mean_square = summed / (HEADS * DK)
     normed = (mixed * lax.rsqrt(mean_square + 1e-06)[:, None] * gain[None, :]).astype(jnp.bfloat16)
     return (normed, final_rows)

time: 93.2 us -> 97.8 us (1.049)
  blocking collectives: 5.83 us -> 10.1 us
  waiting for transfers between devices: 32.7 us -> 31.4 us
    unnamed x0 -> x1, blocking collectives: none -> 10.1 us
    psum x1 -> x0, blocking collectives: 5.83 us -> none  [local(): summed = lax.psum(squares, ('head', 'sub'))]
    all_to_all x1, waiting for transfers between devices: 23.1 us -> 21.8 us  [local(): lax.all_to_all(local_state[None], 'seq', split_axis=2, concat_axis=0, til...]
  transfers between devices with their start and end apart: 2 -> 2, of which waited for: 2 -> 2; matrix products, arithmetic and copies ran while one was open for 20% -> 19% of each run, Pallas kernels for 0% -> 0%
where the time goes in v1:
time: 97.8 us; the launch traced here: 97.4 us
  waiting for transfers between devices  31.4 us (32%)
  matrix products  31 us (32%)
  starting transfers between devices  10.8 us (11%)
  blocking collectives  10.1 us (10%)
  other arithmetic  7.72 us (8%)
  local copies, waits for them, and re-layouts  4.98 us (5%)
  between operations  1.4 us (1%)
    all_to_all x1, waiting for transfers between devices, local(): lax.all_to_all(local_state[None], 'seq', split_axis=2, concat_axis=0, til...  21.8 us
    dot_general x1, matrix products, local(): jnp.einsum('hij,jhd->ihd', weights, value_heads, preferred_element_type=j...  12.4 us
    unnamed x1, blocking collectives  10.1 us
    all_to_all x1, waiting for transfers between devices, local(): lax.all_to_all(prefix_by_block, 'seq', split_axis=0, concat_axis=2, tiled...  9.6 us
    dot_general x1, matrix products, local(): jnp.einsum('ihd,hde->ihe', decayed_query, prefix, precision=lax.Precision...  8.21 us
    all_to_all x1, starting transfers between devices, local(): lax.all_to_all(local_state[None], 'seq', split_axis=2, concat_axis=0, til...  6.35 us
    dot_general x1, matrix products, local(): jnp.einsum('ihd,ihe->hde', scaled_keys, value_heads, preferred_element_ty...  4.7 us
    all_to_all x1, starting transfers between devices, local(): lax.all_to_all(prefix_by_block, 'seq', split_axis=0, concat_axis=2, tiled...  4.42 us
  transfers between devices with their start and end apart: 2, of which 2 were waited for; matrix products, arithmetic and copies ran while one was open for 19% of the time, Pallas kernels for 0%

profile of v1, /device:TPU:0, one launch (start us, length us, event | category | flops | bytes accessed | tf_op | source)
XLA Modules:
  0.0 97.4 jit_solution(1171183307595716769)
XLA Ops:
  0.6 0.0 copy-start
  0.7 0.8 broadcast_multiply_fusion
  1.5 0.1 multiply_exponential_fusion
  1.6 4.7 %fusion.30 = f32[1,16,128,128]{3,2,1,0:T(8,128)S(1)} fusion(f32[576,16]{0,1:T(8,128)S(1)} %get-tuple-element.3, bf16[576,2048]{1,0:T(8,128)(2,1)} %param.7, bf16[576,2048]{1,0:T(8,128)(2,1)} %param.6), kind=kOutput, calls=%fused_computation.30 | convolution fusion | flops 305528832 | bytes 5804032 | tf_op jit(solution)/shard_map/ihd,ihe->hde/dot_general | solution.py:28
  6.3 0.0 copy-start.2
  6.3 1.6 %copy.46 = f32[1,16,128,128]{3,1,0,2:T(8,128)} copy(f32[1,16,128,128]{3,2,1,0:T(8,128)S(1)} %fusion.30) | data formatting | bytes 2097152 | tf_op jit(solution)/shard_map/broadcast_in_dim | solution.py:31
  7.9 6.3 %all-to-all-start = ((f32[1,16,128,128]{3,1,0,2:T(8,128)}), f32[1,16,128,128]{3,1,0,2:T(8,128)S(1)}, u32[]{:S(2)}, u32[]{:S(2)}) async-start(f32[1,16,128,128]{3,1,0,2:T(8,128)} %copy.46), calls=%async_computation | async-start | bytes 2097152 | tf_op jit(solution)/shard_map/all_to_all | solution.py:31
  14.2 0.1 exponential_bitcast_fusion
  14.3 0.1 copy.54
  14.4 0.0 copy-done.2
  14.4 0.6 dynamic-slice
  15.7 0.1 subtract_compare_fusion.1
  15.7 0.1 subtract_maximum_fusion.1
  15.8 1.1 %subtract_compare_fusion = pred[576,576]{1,0:T(8,128)(4,1)} fusion(f32[576]{0:T(1024)S(1)} %iota_convert_fusion), kind=kLoop, calls=%fused_computation.23 | loop fusion | flops 663552 | bytes 334080 | tf_op jit(solution)/shard_map/ge | solution.py:18
  16.9 1.3 %subtract_maximum_fusion = f32[576,576]{1,0:T(8,128)} fusion(f32[576]{0:T(1024)S(1)} %iota_convert_fusion), kind=kLoop, calls=%fused_computation.22 | loop fusion | flops 663552 | bytes 1329408 | tf_op jit(solution)/shard_map/max | solution.py:20
  18.1 21.8 %all-to-all-done = f32[1,16,128,128]{3,1,0,2:T(8,128)S(1)} async-done(((f32[1,16,128,128]{3,1,0,2:T(8,128)}), f32[1,16,128,128]{3,1,0,2:T(8,128)S(1)}, u32[]{:S(2)}, u32[]{:S(2)}) %all-to-all-start) | async-done | bytes 1048608 | tf_op jit(solution)/shard_map/all_to_all | solution.py:31
  39.9 2.5 %convolution_bitcast_fusion = f32[4,16,32,128]{3,0,2,1:T(4,128)S(1)} fusion(f32[1,16,4,32,128]{4,1,3,2,0:T(8,128)S(1)} %bitcast.94, f32[4,4]{1,0:T(4,128)S(1)} %subtract_maximum_fusion.1, f32[16]{0:T(128)S(1)} %get-tuple-element.4, pred[4,4]{1,0:T(4,128)(4,1)S(1)} %subtract_compare_fusion.1), kind=kOutput, calls=%fused_computation.31 | convolution fusion | flops 12583680 | bytes 2097296 | tf_op jit(solution)/shard_map/bmh,mhre->bhre/dot_general | solution.py:40
  42.5 1.1 %copy.49 = f32[4,16,32,128]{3,2,1,0:T(8,128)} copy(f32[4,16,32,128]{3,0,2,1:T(4,128)S(1)} %convolution_bitcast_fusion) | data formatting | bytes 2097152 | tf_op jit(solution)/shard_map/bmh,mhre->bhre/transpose | solution.py:40
  43.6 4.4 %all-to-all-start.1 = ((f32[4,16,32,128]{3,2,1,0:T(8,128)}), f32[4,16,32,128]{3,2,1,0:T(8,128)}, u32[]{:S(2)}, u32[]{:S(2)}) async-start(f32[4,16,32,128]{3,2,1,0:T(8,128)} %copy.49), calls=%async_computation.1 | async-start | bytes 2097152 | tf_op jit(solution)/shard_map/all_to_all | solution.py:44
  48.0 0.0 copy-done
  48.0 12.4 %fusion = f32[16,576,128]{2,1,0:T(8,128)} fusion(f32[576,576]{1,0:T(8,128)} %subtract_maximum_fusion, f32[16]{0:T(128)S(1)} %get-tuple-element.5, pred[576,576]{1,0:T(8,128)(4,1)} %subtract_compare_fusion, bf16[576,2048]{1,0:T(8,128)(2,1)} %param.7, bf16[576,2048]{1,0:T(8,128)(2,1)} %param.6, bf16[576,2048]{1,0:T(8,128)(2,1)S(1)} %copy-done), kind=kOutput, calls=%fused_computation.1 | convolution fusion | flops 2744451072 | bytes 13455424 | tf_op jit(solution)/shard_map/hij,jhd->ihd/dot_general | solution.py:47
  60.5 3.1 %fusion.33 = f32[16,1,32,128]{3,1,2,0:T(1,128)} fusion(f32[4,16,1,1]{0,2,3,1:T(1,128)S(1)} %copy.54, f32[1,16,4,32,128]{4,1,3,2,0:T(8,128)S(1)} %bitcast.95), kind=kOutput, calls=%fused_computation.32 | convolution fusion | flops 3145728 | bytes 1310976 | tf_op jit(solution)/shard_map/mh,mhre->hre/dot_general | solution.py:43
  63.6 9.6 %all-to-all-done.1 = f32[4,16,32,128]{3,2,1,0:T(8,128)} async-done(((f32[4,16,32,128]{3,2,1,0:T(8,128)}), f32[4,16,32,128]{3,2,1,0:T(8,128)}, u32[]{:S(2)}, u32[]{:S(2)}) %all-to-all-start.1) | async-done | bytes 1048608 | tf_op jit(solution)/shard_map/all_to_all | solution.py:44
  73.2 1.3 %copy.50 = f32[4,16,32,128]{3,2,0,1:T(8,128)S(1)} copy(f32[4,16,32,128]{3,2,1,0:T(8,128)} %all-to-all-done.1) | data formatting | bytes 2097152 | tf_op jit(solution)/shard_map/all_to_all | solution.py:44
  74.5 0.0 copy-start.1
  74.5 8.2 %multiply_reduce_fusion = (f32[576]{0:T(1024)S(1)}, f32[576,16,128]{2,0,1:T(8,128)}) fusion(f32[16,128,128]{2,1,0:T(8,128)S(1)} %bitcast.96, f32[576,16]{0,1:T(8,128)S(1)} %get-tuple-element.2, f32[16,576,128]{2,1,0:T(8,128)} %fusion, bf16[576,2048]{1,0:T(8,128)(2,1)S(1)} %copy-done), kind=kOutput, calls=%fused_computation.8 | convolution fusion | flops 1817837056 | bytes 12884224 | tf_op jit(solution)/shard_map/ihd,hde->ihe/dot_general | solution.py:49
  82.7 0.2 dynamic-update-slice
  82.9 10.1 %all-reduce = f32[2304]{0:T(1024)S(1)} all-reduce(f32[2304]{0:T(1024)S(1)} %dynamic-update-slice), channel_id=2, replica_groups=mesh['groups'=2,'seq'=4,'head'=2,'sub'=2] {'head','sub'}, use_global_device_ids=true, to_apply=%add | all-reduce | flops 2304 | bytes 18432
  93.0 0.1 reshape.227
  93.2 0.0 copy-done.1
  93.2 4.2 %fusion.5 = bf16[576,2048]{1,0:T(8,128)(2,1)} fusion(f32[2048]{0:T(1024)S(1)} %copy-done.1, f32[576]{0:T(1024)S(1)} %add_rsqrt_fusion, f32[576,16,128]{2,0,1:T(8,128)} %get-tuple-element.7), kind=kLoop, calls=%fused_computation.6 | loop fusion | flops 3538944 | bytes 7088384 | tf_op jit(solution)/shard_map/convert_element_type | solution.py:55
  (8 shorter events, 0.0 us)
Async XLA Ops:
  0.6 47.4 %copy-start = (bf16[576,2048]{1,0:T(8,128)(2,1)S(1)}, bf16[576,2048]{1,0:T(8,128)(2,1)}, u32[]{:S(2)}) copy-start(bf16[576,2048]{1,0:T(8,128)(2,1)} %param.5) | copy-start | bytes 7077892
  6.3 8.1 %copy-start.2 = (u32[32]{0:T(128)S(1)}, u32[32]{0:T(128)}, u32[]{:S(2)}) copy-start(u32[32]{0:T(128)} %constant.8) | copy-start | bytes 388
  7.9 32.1 %all-to-all-start = ((f32[1,16,128,128]{3,1,0,2:T(8,128)}), f32[1,16,128,128]{3,1,0,2:T(8,128)S(1)}, u32[]{:S(2)}, u32[]{:S(2)}) async-start(f32[1,16,128,128]{3,1,0,2:T(8,128)} %copy.46), calls=%async_computation | async-start | bytes 2097152 | tf_op jit(solution)/shard_map/all_to_all | solution.py:31
  43.6 29.6 %all-to-all-start.1 = ((f32[4,16,32,128]{3,2,1,0:T(8,128)}), f32[4,16,32,128]{3,2,1,0:T(8,128)}, u32[]{:S(2)}, u32[]{:S(2)}) async-start(f32[4,16,32,128]{3,2,1,0:T(8,128)} %copy.49), calls=%async_computation.1 | async-start | bytes 2097152 | tf_op jit(solution)/shard_map/all_to_all | solution.py:44
  74.5 18.7 %copy-start.1 = (f32[2048]{0:T(1024)S(1)}, f32[2048]{0:T(1024)}, u32[]{:S(2)}) copy-start(f32[2048]{0:T(1024)} %param.9) | copy-start | bytes 24580
